TPU v7x, 128 devices: a whole 4x4x4 slice. The times are simulated.
128 devices in a mesh: dp: 16 (over z, y_hi, core), section: 2 (over y_lo), mp: 4 (over x).
Axes of the slice: x: 4, y: 4 (y_hi: 2, y_lo: 2; y = y_hi * 2 + y_lo), z: 4, core: 2. Of those that a mesh axis runs over, the one named last changes fastest.
Arguments:
- patches: bfloat16 [16, 2, 16, 16, 3200], P('dp', 'section'), may hold values from -6 to 6
- w_in: bfloat16 [3200, 3584], P(None, 'mp'), may hold values from -0.109375 to 0.109375
- ln_gain: float32 [3584], P('mp'), may hold values from 0.25 to 1.75
- ln_bias: float32 [3584], P('mp'), may hold values from -3 to 3
- dw_kernel: float32 [3, 3, 3584], P(None, None, 'mp'), may hold values from -2 to 2
- w_tube: bfloat16 [2, 2, 2, 3584, 3584], P('section', None, None, 'mp', 'dp'), may hold values from -0.03125 to 0.03125
- grad_out: bfloat16 [16, 64, 3584], P(None, None, 'dp'), may hold values from -6 to 6
- clip_frames: int32 [16], replicated, may hold values from 8 to 32, as said below
- clip_batch: int32 [16], replicated, may hold values from 0 to 3
Outputs:
- tubes: bfloat16 [16, 64, 3584], P(None, ('section', 'mp'), 'dp')
- grad_w_in: float32 [3200, 3584], P(None, ('mp', 'dp', 'section'))
- grad_gain: float32 [3584], P(('mp', 'dp', 'section'))
- grad_bias: float32 [3584], P(('mp', 'dp', 'section'))
- grad_dw: float32 [3, 3, 3584], P(None, None, ('mp', 'dp', 'section'))
- grad_w_tube: float32 [2, 2, 2, 3584, 3584], P('section', None, None, 'mp', 'dp')
Inputs may be any that keep to these rules, and one draw needn't show every extreme that they name: `clip_frames`: even numbers; their halves sum to 16 or more.
All inputs are finite; a program needn't handle non-finite values.
Results may differ from a plain program's by a relative error of at most 0.005.
Values may be sent and summed in bfloat16 or wider, within the bound.
A program may use at most 128 MiB of HBM per device.

v0:
```python
import jax
import jax.numpy as jnp
from jax import lax
from jax.experimental import pallas as pl
from jax.experimental.pallas import tpu as pltpu
from jax.sharding import PartitionSpec as P

MESH = pl.DeviceIdType.MESH
F32 = jnp.float32
BF16 = jnp.bfloat16

CH = 3584
EPS = 1e-06
W = 896
D = 3200
OW = 224
TOK = 256
DX = D + 128
HX = DX // 2
LANES = 128
NB = W // LANES


class Place:
    def __init__(self):
        dp = lax.axis_index("dp")
        self.z = dp // 4
        self.yh = (dp // 2) % 2
        self.core = dp % 2
        self.sec = lax.axis_index("section")
        self.mp = lax.axis_index("mp")
        self.y = self.yh * 2 + self.sec

    def at(self, z, yh, core):
        return (z * 4 + yh * 2 + core, self.sec, self.mp)

    def zmove(self, k):
        return self.at((self.z + k) % 4, self.yh, self.core)

    def partner(self):
        return self.at(self.z, self.yh, 1 - self.core)

    def yhflip(self):
        return self.at(self.z, 1 - self.yh, self.core)

    def ymove(self, k):
        y = (self.y + k) % 4
        return (self.z * 4 + (y // 2) * 2 + self.core, y % 2, self.mp)

    def mpmove(self, k):
        return (self.z * 4 + self.yh * 2 + self.core, self.sec, (self.mp + k) % 4)


def greet(devices):
    barrier = pltpu.get_barrier_semaphore()
    for dev in devices:
        pl.semaphore_signal(barrier, inc=1, device_id=dev, device_id_type=MESH)
    pl.semaphore_wait(barrier, len(devices))


def remote(src, dst, send, recv, dev):
    return pltpu.make_async_remote_copy(
        src_ref=src, dst_ref=dst, send_sem=send, recv_sem=recv, device_id=dev, device_id_type=MESH
    )


def lanes(b):
    return pl.ds(pl.multiple_of(b * LANES, LANES), LANES)


def sigmoid(v):
    return 1.0 / (1.0 + jnp.exp(-v))


def shift_j(plane, d):
    if d == 0:
        return plane
    row = lax.broadcasted_iota(jnp.int32, plane.shape, 0) % 8
    if d < 0:
        return jnp.where(row == 0, 0.0, pltpu.roll(plane, 1, 0))
    return jnp.where(row == 7, 0.0, pltpu.roll(plane, plane.shape[0] - 1, 0))


def shift_i(plane, d):
    if d == 0:
        return plane
    blank = jnp.zeros((8, plane.shape[1]), plane.dtype)
    if d < 0:
        return jnp.concatenate([blank, plane[:-8]], axis=0)
    return jnp.concatenate([plane[8:], blank], axis=0)


def neighbours(planes):
    moved = {}

    def get(s, t):
        us, di = s % 2, s // 2
        vs, dj = t % 2, t // 2
        if (us, vs, dj) not in moved:
            moved[us, vs, dj] = shift_j(planes[us][vs], dj)
        return shift_i(moved[us, vs, dj], di)

    return get


def across(rows, width):
    return jnp.transpose(rows)[:width]


def down(row):
    return jnp.transpose(jnp.broadcast_to(row, (LANES, row.shape[1])))


def lane_sum(x):
    return jnp.sum(x, axis=1, keepdims=True)


def two_parts(x):
    full = x + pltpu.roll(x, 64, 1)
    high = full.astype(BF16).astype(F32)
    lane = lax.broadcasted_iota(jnp.int32, x.shape, 1)
    return jnp.where(lane < 64, high, full - high).astype(BF16)


def to_link(x, grad):
    if grad == x.shape[1]:
        return x.astype(BF16)
    return jnp.concatenate([x[:, :grad].astype(BF16), two_parts(x[:, grad:])], axis=1)


def pick_lane(first, second):
    lane = lax.broadcasted_iota(jnp.int32, (TOK, LANES), 1)
    return jnp.where(lane == 0, first, jnp.where(lane == 1, second, 0.0))


VMEM = pl.BlockSpec(memory_space=pltpu.VMEM)
ANY = pl.BlockSpec(memory_space=pl.ANY)
SMEM = pl.BlockSpec(memory_space=pltpu.SMEM)
DMA = pltpu.SemaphoreType.DMA


PIECES = ((0, 0, 896), (1, 896, 896), (1, 1792, 768), (1, 2560, 768))
GROUPS = (0, 3, 1, 2)
NSEM = 128


def ds(start, size, align):
    return pl.ds(pl.multiple_of(start, align), size)


def main_kernel(
    frames, batch, patches, w_in, wt, gout, gain1, bias1, dw,
    tubes, gwin, gdw, ggain, gbias, gwt,
    pv, pp, wv, wtv, wto, gov, goo, wrow, upr, upo, gain, bias,
    sa, ra, part, sb, rb, own, sc, rc, rya, ryc,
    pre, normed, act, slope, mslope, gmaps, small, stat, stat2,
    ev, sub, gp, left, leftr,
    ra2, rb2, own2, ownb, tra, tb, trb, acc, upt, ts, tr,
    load, send, recv,
):
    me = Place()
    loads = [
        pltpu.make_async_copy(gout, gov, load.at[0]),
        pltpu.make_async_copy(wt, wtv, load.at[1]),
        pltpu.make_async_copy(patches, pv, load.at[2]),
        pltpu.make_async_copy(w_in, wv, load.at[3]),
    ]
    for copy in loads:
        copy.start()
    mate = me.partner()
    zs = (me.zmove(1), me.zmove(3))
    ys = (me.ymove(1), me.ymove(3))
    mpk = [me.mpmove(k) for k in (1, 2, 3)]
    dest = me.sec * 4 + me.mp
    peers = []
    for k in range(1, 8):
        d = (dest + k) % 8
        peers.append((d, (lax.axis_index("dp"), d // 4, d % 4)))
    greet([mate, *zs, *ys, *[dev for _, dev in peers]])
    pending, number = [], {}

    def go(name, src, dst, dev):
        i = number.setdefault(name, len(number))
        copy = remote(src, dst, send.at[i], recv.at[i], dev)
        copy.start()
        pending.append(copy)
        return copy

    got_gout = go("gout", gout, goo, mate)
    got_wt = go("wt", wt, wto, mate)

    clip = lax.broadcasted_iota(jnp.int32, (16, 16), 0)
    other = lax.broadcasted_iota(jnp.int32, (16, 16), 1)
    zero = jnp.zeros((16, 16), jnp.int32)
    half_c, half_r, bat_c, bat_r = zero, zero, zero, zero
    for k in range(16):
        half_c = jnp.where(clip == k, frames[k], half_c)
        half_r = jnp.where(other == k, frames[k], half_r)
        bat_c = jnp.where(clip == k, batch[k], bat_c)
        bat_r = jnp.where(other == k, batch[k], bat_r)
    half_c = half_c.astype(F32) * 0.5
    half_r = half_r.astype(F32) * 0.5
    ends = jnp.sum(jnp.where(clip <= other, half_c, 0.0), axis=0, keepdims=True)
    starts = ends - half_r
    held = jnp.sum(jnp.where(bat_c == bat_r, half_c, 0.0), axis=0, keepdims=True)
    scale = (10.0 * 16) / (4.0 * held)
    place = clip.astype(F32)
    member = (place >= starts) & (place < ends)
    weight = jnp.sum(jnp.where(member, scale, 0.0), axis=1, keepdims=True)
    wrow[...] = jnp.broadcast_to(weight, (16, OW))
    gain[...] = gain1[...].reshape(1, W)
    bias[...] = bias1[...].reshape(1, W)

    r = lax.broadcasted_iota(jnp.int32, (TOK, TOK), 0)
    t = lax.broadcasted_iota(jnp.int32, (TOK, TOK), 1)
    token = (2 * ((r // 8) % 8) + r // 128) * 16 + 2 * (r % 8) + (r // 64) % 2
    order = jnp.where(token == t, 1.0, 0.0).astype(BF16)

    def pair_of(slot):
        zr, yr, cr = slot // 4, (slot // 2) % 2, slot % 2
        yh = me.yh if yr == 0 else 1 - me.yh
        core = me.core if cr == 0 else 1 - me.core
        return ((me.z + zr) % 4) * 4 + yh * 2 + core

    loads[0].wait()
    for slot in range(16):
        p = pair_of(slot)
        upr[64 * slot : 64 * slot + 64] = (gov[p].astype(F32) * wrow[pl.ds(p, 1), :]).astype(BF16)
    loads[2].wait()

    @pl.loop(0, 5)
    def _(k):
        cols = ds(k * 640, 640, LANES)
        pp[0, :, cols] = jnp.dot(order, pv[:, cols], preferred_element_type=F32).astype(BF16)

    got_gout.wait_recv()
    for k in range(4):
        for q in range(2):
            p = pair_of(4 * k + 2 - 2 * q)
            upo[k, 64 * q : 64 * q + 64] = (goo[p].astype(F32) * wrow[pl.ds(p, 1), :]).astype(BF16)
    loads[1].wait()
    got_wt.wait_recv()

    def term(k, uv):
        mine = jnp.concatenate([upr[256 * k + 128 : 256 * k + 192], upr[256 * k : 256 * k + 64]], axis=0)
        return jnp.dot(mine, wtv[uv], preferred_element_type=F32) + jnp.dot(
            upo[k], wto[uv], preferred_element_type=F32
        )

    @pl.loop(0, 4)
    def _(uv):
        res = term(2, uv).astype(BF16)
        sa[0, uv] = res[:64]
        sa[1, uv] = res[64:]

    U = (slice(0, 2), slice(2, 4))

    def send_a(q):
        return [go(f"a{q}{s}", sa.at[q, U[s]], ra.at[q, U[s]], zs[s]) for s in range(2)]

    def send_b(q, s, half):
        return go(f"b{q}{s}{half}", sb.at[s, q, U[half]], rb.at[s, q, U[half]], zs[s])

    got_a = [send_a(0), None]

    @pl.loop(0, 2)
    def _(k):
        for s, step in enumerate((1, 3)):
            res = term(step, 2 * s + k)
            part[s, 0, k] = res[:64]
            part[s, 1, k] = res[64:]
            res = term(step, 2 - 2 * s + k).astype(BF16)
            sb[s, 0, 2 - 2 * s + k] = res[:64]
            sb[s, 1, 2 - 2 * s + k] = res[64:]

    got_b = [[], []]
    got_b[0] += [send_b(0, s, 1 - s) for s in range(2)]

    def add_a(q):
        for s in range(2):
            got_a[q][s].wait_recv()
            sb[s, q, U[s]] = (part[s, q] + ra[q, U[s]].astype(F32)).astype(BF16)
            got_b[q].append(send_b(q, s, s))

    loads[3].wait()
    pre[...] = jnp.dot(pp[0], wv[...], preferred_element_type=F32)

    total = pre[:, 0:LANES]
    for b in range(1, NB):
        total = total + pre[:, b * LANES : (b + 1) * LANES]
    mean = lane_sum(total) * (1.0 / W)
    total = jnp.zeros((TOK, LANES), F32)
    for b in range(NB):
        dev = pre[:, b * LANES : (b + 1) * LANES] - mean
        total = total + dev * dev
    stat[0] = across(pick_lane(mean, lane_sum(total)), 8)
    got_stat = [go(f"stat{k}", stat.at[0], stat.at[k], mpk[k - 1]) for k in (1, 2, 3)]

    add_a(0)
    got_a[1] = send_a(1)
    got_b[1] += [send_b(1, s, 1 - s) for s in range(2)]

    @pl.loop(0, 4)
    def _(uv):
        res = term(0, uv)
        own[0, uv] = res[:64]
        own[1, uv] = res[64:]

    for copy in got_stat:
        copy.wait_recv()
    means = [stat[k][0:1] for k in range(4)]
    mean = (means[0] + means[1] + means[2] + means[3]) * 0.25
    var = stat[0][1:2] + stat[1][1:2] + stat[2][1:2] + stat[3][1:2]
    for m in means:
        var = var + W * (m - mean) * (m - mean)
    rs = down(lax.rsqrt(var * (1.0 / CH) + EPS))
    mu = down(mean)

    def cut(x):
        return [[x[128 * u + 64 * v : 128 * u + 64 * v + 64] for v in (0, 1)] for u in (0, 1)]

    @pl.loop(0, NB)
    def _(b):
        cols = lanes(b)
        norm = (pre[:, cols] - mu) * rs
        normed[:, cols] = norm
        shifted = norm * gain[:, cols] + bias[:, cols]
        sig = sigmoid(shifted)
        av = shifted * sig
        act[:, cols] = av
        slope[:, cols] = sig * (1.0 + shifted * (1.0 - sig))
        avc = cut(av)
        get = neighbours(avc)
        for u in range(2):
            for v in range(2):
                mix = jnp.zeros((64, LANES), F32)
                for a in range(3):
                    for c in range(3):
                        mix = mix + dw[a, c : c + 1, cols] * get(u + a - 1, v + c - 1)
                ms = sigmoid(mix)
                mslope[pl.ds(128 * u + 64 * v, 64), cols] = ms * (1.0 + mix * (1.0 - ms))
                ev[2 * u + v, 0:64, cols] = (avc[u][v] + mix * ms).astype(BF16)

    def spot(slot, half=None):
        return ev.at[slice(0, 4) if half is None else U[half], 64 * slot : 64 * slot + 64]

    def to_mate(slot, half=None):
        return go(f"m{slot}{half}", spot(slot, half), spot(slot + 1, half), mate)

    def over_y(name, src, relay):
        return [go(f"{name}{s}", src(s), relay.at[s], ys[s]) for s in range(2)]

    def pass_y(name, got, relay, dst):
        out = []
        for s in range(2):
            got[s].wait_recv()
            out.append(go(f"{name}p{s}", relay.at[s], dst(s), ys[s]))
        return out

    got_ya = over_y("ya", lambda s: spot(0, s), rya)
    got_mate = [to_mate(0)]

    for copy in got_b[0]:
        copy.wait_recv()
    sc[...] = (own[0] + rb[0, 0].astype(F32) + rb[1, 0].astype(F32)).astype(BF16)
    got_yc = over_y("yc", lambda s: sc.at[U[s]], ryc)
    got_flip = pass_y("ya", got_ya, rya, lambda s: spot(2, s))
    add_a(1)

    def spread(slot):
        return [
            go(f"z{slot}0", spot(slot), spot(slot + 12), zs[0]),
            go(f"z{slot}1", spot(slot), spot(slot + 4), zs[1]),
        ]

    got_z = spread(0)
    got_pp = go("pp", pp.at[0], pp.at[1], mate)

    r = lax.broadcasted_iota(jnp.int32, (512, W), 0)
    ch = lax.broadcasted_iota(jnp.int32, (512, W), 1)
    group, k = r // 32, r % 32
    base = ((group // 4) * 4 + ((group // 2) % 2) * 2) * 56 + (group % 2) * 28 + k
    base = jnp.where(k < 28, base, -10000)
    for s in range(2):
        core = me.core if s == 0 else 1 - me.core
        sub[s] = jnp.where(base + core * 56 == ch, 1.0, 0.0).astype(BF16)
    upt[...] = jnp.transpose(upr[...].astype(F32)).astype(BF16)

    got_c = pass_y("yc", got_yc, ryc, lambda s: rc.at[U[s]])
    for copy in got_flip:
        copy.wait_recv()
    got_zf = spread(2)
    got_mate.append(to_mate(2))

    for copy in got_b[1]:
        copy.wait_recv()
    for uv in range(4):
        own[1, uv] = own[1, uv] + rb[0, 1, uv].astype(F32) + rb[1, 1, uv].astype(F32)
    for copy in got_c:
        copy.wait_recv()
    for uv in range(4):
        gmaps[64 * uv : 64 * uv + 64, :] = own[1, uv] + rc[uv].astype(F32)

    @pl.loop(0, NB)
    def _(b):
        cols = lanes(b)
        norm = normed[:, cols]
        gm = gmaps[:, cols]
        gmc, avc = cut(gm * mslope[:, cols]), cut(act[:, cols])
        get, geta = neighbours(gmc), neighbours(avc)
        slo = slope[:, cols]
        dws = [[dw[a, c : c + 1, cols] for c in range(3)] for a in range(3)]
        gain_sum = jnp.zeros((64, LANES), F32)
        bias_sum = jnp.zeros((64, LANES), F32)
        for u in range(2):
            for v in range(2):
                at = slice(128 * u + 64 * v, 128 * u + 64 * v + 64)
                ga = gm[at]
                for a in range(3):
                    for c in range(3):
                        ga = ga + dws[a][c] * get(u + 1 - a, v + 1 - c)
                gs = ga * slo[at]
                bias_sum = bias_sum + gs
                gain_sum = gain_sum + gs * norm[at]
                pre[pl.ds(128 * u + 64 * v, 64), cols] = gs * gain[:, cols]
        for a in range(3):
            for c in range(3):
                tot = jnp.zeros((64, LANES), F32)
                for u in range(2):
                    for v in range(2):
                        tot = tot + gmc[u][v] * geta(u + a - 1, v + c - 1)
                k = 3 * a + c
                small[k : k + 1, cols] = jnp.sum(tot, axis=0, keepdims=True)
        small[9:10, cols] = jnp.sum(gain_sum, axis=0, keepdims=True)
        small[10:11, cols] = jnp.sum(bias_sum, axis=0, keepdims=True)

    one = jnp.zeros((TOK, LANES), F32)
    two = jnp.zeros((TOK, LANES), F32)
    for b in range(NB):
        g = pre[:, b * LANES : (b + 1) * LANES]
        one = one + g
        two = two + g * normed[:, b * LANES : (b + 1) * LANES]
    stat2[0] = across(pick_lane(lane_sum(one), lane_sum(two)), 8)
    got_stat = [go(f"back{k}", stat2.at[0], stat2.at[k], mpk[k - 1]) for k in (1, 2, 3)]

    def onward(slot, got):
        out = []
        got[0].wait_recv()
        out.append(go(f"f{slot}0", spot(slot + 12, 0), spot(slot + 8, 0), zs[0]))
        got_mate.append(to_mate(slot + 12))
        got[1].wait_recv()
        out.append(go(f"f{slot}1", spot(slot + 4, 1), spot(slot + 8, 1), zs[1]))
        got_mate.append(to_mate(slot + 4))
        return out

    def gather_end(slot, got):
        for s in range(2):
            got[s].wait_recv()
            got_mate.append(to_mate(slot + 8, s))

    got_f = onward(0, got_z)

    def products(n, first):
        rows = slice(256 * n, 256 * n + 256)

        @pl.loop(0, 4)
        def _(uv):
            res = lax.dot_general(
                ev[uv, rows], wtv[uv], (((1,), (1,)), ((), ())), preferred_element_type=F32
            )

            @pl.when(uv == 0)
            def _():
                acc[rows] = res

            @pl.when(uv > 0)
            def _():
                acc[rows] = acc[rows] + res

            more = jnp.dot(upt[:, rows], ev[uv, rows], preferred_element_type=F32)
            gwt[uv] = more if first else gwt[uv] + more

    for copy in got_mate[:2]:
        copy.wait_recv()
    products(0, True)

    for copy in got_stat:
        copy.wait_recv()
    total = stat2[0] + stat2[1] + stat2[2] + stat2[3]
    m1 = down(total[0:1] * (1.0 / CH))
    m2 = down(total[1:2] * (1.0 / CH))

    @pl.loop(0, NB)
    def _(b):
        cols = lanes(b)
        out = (pre[:, cols] - m1 - normed[:, cols] * m2) * rs
        gp[0:TOK, cols] = out.astype(BF16)
        row = lax.broadcasted_iota(jnp.int32, (16, LANES), 0)
        val = jnp.where(row < 11, small[:, cols], 0.0)
        high = val.astype(BF16)
        gp[TOK : TOK + 16, cols] = high
        gp[TOK + 64 : TOK + 80, cols] = (val - high.astype(F32)).astype(BF16)

    for at in (16, 80):
        gp[TOK + at : TOK + at + 48, :] = jnp.zeros((48, W), BF16)

    def turn(s):
        return lax.dot_general(
            sub[s], gp[...], (((1,), (1,)), ((), ())), preferred_element_type=F32
        ).astype(BF16)

    left[1] = turn(1)
    got_left = go("left", left.at[1], leftr, mate)
    left[0] = turn(0)
    got_pp.wait_recv()
    got_left.wait_recv()

    coord = (me.z, me.y)
    move = (zs, ys)
    got1, got2, got3, got4 = {}, {}, {}, {}

    def gw_at(k, start, size):
        return wv.at[ds(512 * k + start, size, 32), 0 : PIECES[k][2]]

    def sb_at(k, s, b, size):
        return wv.at[2048 + 128 * k + 64 * s + b : 2048 + 128 * k + 64 * s + b + size, 0 : PIECES[k][2]]

    def stage1(k):
        h, first, n = PIECES[k]
        grad = min(first + n, D) - first
        res = jnp.dot(left[0, :, 0:TOK], pp[0, :, first : first + grad], preferred_element_type=F32)
        res = res + jnp.dot(leftr[:, 0:TOK], pp[1, :, first : first + grad], preferred_element_type=F32)
        if grad < n:
            tail = left[0, :, TOK : TOK + LANES].astype(F32) + leftr[:, TOK : TOK + LANES].astype(F32)
            res = jnp.concatenate([res, tail], axis=1)
        res = to_link(res, grad)
        if h == 0:
            wv[512 * k : 512 * k + 512, 0:n] = res
        else:
            for a in range(4):
                for b in range(4):
                    to = 512 * k + 32 * (4 * a + b)
                    wv[to : to + 32, 0:n] = res[32 * (4 * b + a) : 32 * (4 * b + a) + 32]
        far = 128 * ((coord[h] + 2) % 4)
        got1[k] = [
            go(f"A{k}{s}", gw_at(k, far + 64 * s, 64), ra2.at[k, 64 * s : 64 * s + 64, 0:n], move[h][s])
            for s in range(2)
        ]
        got2[k] = []
        for s in range(2):
            near = 128 * ((coord[h] + 1 + 2 * s) % 4)
            rows = slice(64 - 64 * s, 128 - 64 * s)
            got2[k].append(
                go(f"B{k}{s}", gw_at(k, near + 64 - 64 * s, 64), rb2.at[k, s, rows, 0:n], move[h][s])
            )

    def stage2(k):
        h, first, n = PIECES[k]
        grad = min(first + n, D) - first
        for s in range(2):
            near = 128 * ((coord[h] + 1 + 2 * s) % 4)
            rows = slice(64 * s, 64 * s + 64)
            got1[k][s].wait_recv()
            to = sb_at(k, s, 0, 64)
            val = gw_at(k, near + 64 * s, 64)[...].astype(F32) + ra2[k, rows, 0:n].astype(F32)
            to[...] = to_link(val, grad)
            got2[k].append(go(f"C{k}{s}", to, rb2.at[k, s, rows, 0:n], move[h][s]))

    def stage3(k):
        h, first, n = PIECES[k]
        o = 1 - h
        for copy in got2[k]:
            copy.wait_recv()
        val = gw_at(k, 128 * coord[h], 128)[...].astype(F32)
        val = val + rb2[k, 0, :, 0:n].astype(F32) + rb2[k, 1, :, 0:n].astype(F32)
        own2[k, :, 0:n] = val
        ownb[k, :, 0:n] = to_link(val, min(first + n, D) - first)
        far = 32 * ((coord[o] + 2) % 4)
        got3[k] = [
            go(
                f"D{k}{s}", ownb.at[k, ds(far + 16 * s, 16, 16), 0:n],
                tra.at[k, 16 * s : 16 * s + 16, 0:n], move[o][s],
            )
            for s in range(2)
        ]
        got4[k] = []
        for s in range(2):
            near = 32 * ((coord[o] + 1 + 2 * s) % 4)
            rows = slice(16 - 16 * s, 32 - 16 * s)
            got4[k].append(
                go(
                    f"E{k}{s}", ownb.at[k, ds(near + 16 - 16 * s, 16, 16), 0:n],
                    trb.at[k, s, rows, 0:n], move[o][s],
                )
            )

    def stage4(k):
        h, first, n = PIECES[k]
        o = 1 - h
        for s in range(2):
            near = 32 * ((coord[o] + 1 + 2 * s) % 4)
            rows = slice(16 * s, 16 * s + 16)
            got3[k][s].wait_recv()
            val = own2[k, ds(near + 16 * s, 16, 16), 0:n] + tra[k, rows, 0:n].astype(F32)
            tb[k, s, :, 0:n] = to_link(val, min(first + n, D) - first)
            got4[k].append(go(f"F{k}{s}", tb.at[k, s, :, 0:n], trb.at[k, s, rows, 0:n], move[o][s]))

    def stage5(k):
        h, first, n = PIECES[k]
        for copy in got4[k]:
            copy.wait_recv()
        val = own2[k, ds(32 * coord[1 - h], 32, 32), 0:n]
        val = val + trb[k, 0, :, 0:n].astype(F32) + trb[k, 1, :, 0:n].astype(F32)
        grad = min(first + n, D) - first
        gwin[:, first : first + grad] = val[0:28, 0:grad]
        if grad < n:
            tail = jnp.transpose(jnp.concatenate([val[:, grad:], jnp.zeros((96, LANES), F32)], axis=0))
            tail = tail[0:16] + tail[64:80]
            for a in range(3):
                gdw[a] = tail[3 * a : 3 * a + 3, 0:28]
            ggain[...] = tail[9:10, 0:28]
            gbias[...] = tail[10:11, 0:28]

    for k in range(4):
        stage1(k)
    gather_end(0, got_f)
    got_ff = onward(2, got_zf)
    for k in range(4):
        stage2(k)
    for copy in got_mate[2:8]:
        copy.wait_recv()
    products(3, False)
    products(1, False)
    stage3(0)
    stage3(1)
    gather_end(2, got_ff)
    stage3(2)
    stage4(0)
    stage4(1)
    for copy in got_mate[8:]:
        copy.wait_recv()
    products(2, False)

    for k in range(8):
        piece = jnp.concatenate([acc[64 * s + 8 * k : 64 * s + 8 * k + 8] for s in range(16)], axis=0)
        ts[k] = piece.astype(BF16)
    got_t = [go(f"t{k}", ts.at[d], tr.at[k], dev) for k, (d, dev) in enumerate(peers)]
    stage3(3)
    stage4(2)
    stage5(0)
    stage5(1)
    stage4(3)
    for copy in got_t:
        copy.wait_recv()
    tot = ts[dest].astype(F32)
    for k in range(7):
        tot = tot + tr[k].astype(F32)
    for s in range(16):
        tubes[pair_of(s)] = tot[8 * s : 8 * s + 8].astype(BF16)
    stage5(2)
    stage5(3)
    for copy in pending:
        copy.wait_send()


def run_main(frames, batch, patches, w_in, wt, gout, gain, bias, dw):
    sds = jax.ShapeDtypeStruct
    vm = pltpu.VMEM
    blk, half = (4, 64, W), (2, 64, W)
    return pl.pallas_call(
        main_kernel,
        out_shape=(
            sds((16, 8, OW), BF16), sds((28, D), F32), sds((3, 3, 28), F32),
            sds((1, 28), F32), sds((1, 28), F32), sds((4, OW, W), F32),
        ),
        in_specs=[SMEM, SMEM, ANY, ANY, ANY, ANY, VMEM, VMEM, VMEM],
        out_specs=(VMEM,) * 6,
        scratch_shapes=[
            vm((TOK, D), BF16), vm((2, TOK, D), BF16), vm((D, W), BF16),
            vm((4, OW, W), BF16), vm((4, OW, W), BF16),
            vm((16, 64, OW), BF16), vm((16, 64, OW), BF16), vm((16, OW), F32),
            vm((1024, OW), BF16), vm((4, 128, OW), BF16), vm((1, W), F32), vm((1, W), F32),
            vm((2, *blk), BF16), vm((2, *blk), BF16), vm((2, 2, *half), F32),
            vm((2, 2, *blk), BF16), vm((2, 2, *blk), BF16), vm((2, *blk), F32),
            vm(blk, BF16), vm(blk, BF16), vm((2, *half), BF16), vm((2, *half), BF16),
            *[vm((TOK, W), F32)] * 6, vm((16, W), F32), vm((4, 8, TOK), F32), vm((4, 8, TOK), F32),
            vm((4, 1024, W), BF16), vm((2, 512, W), BF16), vm((TOK + LANES, W), BF16),
            vm((2, 512, TOK + LANES), BF16), vm((512, TOK + LANES), BF16),
            vm((4, 128, W), BF16), vm((4, 2, 128, W), BF16), vm((4, 128, W), F32),
            vm((4, 128, W), BF16), vm((4, 32, W), BF16), vm((4, 2, 16, W), BF16),
            vm((4, 2, 32, W), BF16), vm((1024, OW), F32), vm((OW, 1024), BF16),
            vm((8, 128, OW), BF16), vm((7, 128, OW), BF16),
            DMA((4,)), DMA((NSEM,)), DMA((NSEM,)),
        ],
        compiler_params=pltpu.CompilerParams(
            collective_id=0, has_side_effects=True, vmem_limit_bytes=63 * 1024 * 1024
        ),
        name="main",
    )(frames, batch, patches, w_in, wt, gout, gain, bias, dw)


def out_kernel(a, b, c, d, e, big, ao, bo, co, do, eo, bigo, buf, sem):
    ins = [pltpu.make_async_copy(big.at[k], buf.at[k], sem.at[0, k]) for k in range(4)]
    outs = [pltpu.make_async_copy(buf.at[k], bigo.at[k], sem.at[1, k]) for k in range(4)]
    for copy in ins:
        copy.start()
    for src, dst in ((a, ao), (b, bo), (c, co)):
        dst[...] = src[...]
    do[...] = d[...].reshape(28)
    eo[...] = e[...].reshape(28)
    for k in range(4):
        ins[k].wait()
        outs[k].start()
    for k in range(4):
        outs[k].wait()


def run_out(*arrays):
    sds = jax.ShapeDtypeStruct
    shapes = [sds(x.shape, x.dtype) for x in arrays]
    shapes[3] = shapes[4] = sds((28,), F32)
    return pl.pallas_call(
        out_kernel,
        out_shape=tuple(shapes),
        in_specs=[VMEM] * 5 + [ANY],
        out_specs=tuple([VMEM] * 5 + [ANY]),
        scratch_shapes=[pltpu.VMEM((4, OW, W), F32), DMA((2, 4))],
        name="out",
    )(*arrays)


def shards(patches, w_in, ln_gain, ln_bias, dw_kernel, w_tube, grad_out, clip_frames, clip_batch):
    wt = w_tube.transpose(0, 1, 2, 4, 3).reshape(4, OW, W)
    outs = run_main(
        clip_frames, clip_batch, patches.reshape(TOK, D), w_in, wt, grad_out, ln_gain, ln_bias, dw_kernel
    )
    tubes, gwin, gdw, ggain, gbias, gwt = run_out(*outs)
    return (
        tubes, gwin.T, ggain, gbias, gdw,
        gwt.reshape(1, 2, 2, OW, W).transpose(0, 1, 2, 4, 3),
    )


def solution(mesh):
    placed = (
        P("dp", "section", None, None, None),
        P(None, "mp"),
        P("mp"),
        P("mp"),
        P(None, None, "mp"),
        P("section", None, None, "mp", "dp"),
        P(None, None, "dp"),
        P(),
        P(),
    )
    return jax.shard_map(
        shards,
        mesh=mesh,
        in_specs=placed,
        out_specs=(
            P(None, ("section", "mp"), "dp"),
            P(None, ("mp", "dp", "section")),
            P(("mp", "dp", "section")),
            P(("mp", "dp", "section")),
            P(None, None, ("mp", "dp", "section")),
            P("section", None, None, "mp", "dp"),
        ),
        check_vma=False,
    )
```

profile of v0, /device:TPU:0, one launch (start us, length us, event | category | flops | bytes accessed | tf_op | source)
XLA Modules:
  0.0 107.4 jit_solution(15878877398104300251)
XLA Ops:
  0.6 102.1 %main.1 = (bf16[16,8,224]{2,1,0:T(8,128)(2,1)}, f32[28,3200]{1,0:T(8,128)}, f32[3,3,28]{2,1,0:T(4,128)}, f32[1,28]{1,0:T(1,128)}, f32[1,28]{1,0:T(1,128)}, /*index=5*/f32[4,224,896]{2,1,0:T(8,128)}) custom-call(s32[16]{0:T(128)} %frames.1, s32[16]{0:T(128)} %batch.1, bf16[256,3200]{1,0:T(8,128)(2,1)} %bitcast.8, bf16[3200,896]{1,0:T(8,128)(2,1)} %w_in.1, ...), custom_call_target="tpu_custom_call" | custom-call | tf_op jit(solution)/shard_map/main/pallas_call | solution.py:670
  102.7 4.7 %out.1 = (bf16[16,8,224]{2,1,0:T(8,128)(2,1)}, f32[28,3200]{1,0:T(8,128)}, f32[3,3,28]{2,1,0:T(4,128)}, f32[28]{0:T(128)}, f32[28]{0:T(128)}, /*index=5*/f32[4,224,896]{2,1,0:T(8,128)}) custom-call(bf16[16,8,224]{2,1,0:T(8,128)(2,1)} %get-tuple-element.18.a, f32[28,3200]{1,0:T(8,128)} %get-tuple-element.19.b, f32[3,3,28]{2,1,0:T(4,128)} %get-tuple-element.20.c, ...), custom_call_target="tpu_custom_call" | custom-call | tf_op jit(solution)/shard_map/out/pallas_call | solution.py:722
where the time goes:
time: 108 us; the launch traced here: 107 us
  Pallas kernels  107 us (99%)
    pallas_call x1, Pallas kernels, run_main(): pl.pallas_call(main_kernel, out_shape=(sds((16, 8, OW), BF16), sds((28, D...  102 us
    pallas_call x1, Pallas kernels, run_out(): pl.pallas_call(out_kernel, out_shape=tuple(shapes), in_specs=[VMEM] * 5 +...  4.66 us

commit v1 on v0

--- a/solution.py
+++ b/solution.py
@@ -152,10 +152,10 @@
     frames, batch, patches, w_in, wt, gout, gain1, bias1, dw,
     tubes, gwin, gdw, ggain, gbias, gwt,
     pv, pp, wv, wtv, wto, gov, goo, wrow, upr, upo, gain, bias,
-    sa, ra, part, sb, rb, own, sc, rc, rya, ryc,
+    sf, rf, farp, sa, ra, part, sb, rb, own, sc, rc, rya, ryc, ryf,
     pre, normed, act, slope, mslope, gmaps, small, stat, stat2,
     ev, sub, gp, left, leftr,
-    ra2, rb2, own2, ownb, tra, tb, trb, acc, upt, ts, tr,
+    ra2, rb2, own2, ownb, tra, tb, trb, acc, gacc, upt, ts, tr,
     load, send, recv,
 ):
     me = Place()
@@ -187,7 +187,7 @@
         return copy
 
     got_gout = go("gout", gout, goo, mate)
-    got_wt = go("wt", wt, wto, mate)
+    got_wt = [go(f"wt{k}", wt.at[k], wto.at[k], mate) for k in range(4)]
 
     clip = lax.broadcasted_iota(jnp.int32, (16, 16), 0)
     other = lax.broadcasted_iota(jnp.int32, (16, 16), 1)
@@ -239,7 +239,6 @@
             p = pair_of(4 * k + 2 - 2 * q)
             upo[k, 64 * q : 64 * q + 64] = (goo[p].astype(F32) * wrow[pl.ds(p, 1), :]).astype(BF16)
     loads[1].wait()
-    got_wt.wait_recv()
 
     def term(k, uv):
         mine = jnp.concatenate([upr[256 * k + 128 : 256 * k + 192], upr[256 * k : 256 * k + 64]], axis=0)
@@ -247,40 +246,41 @@
             upo[k], wto[uv], preferred_element_type=F32
         )
 
-    @pl.loop(0, 4)
-    def _(uv):
-        res = term(2, uv).astype(BF16)
-        sa[0, uv] = res[:64]
-        sa[1, uv] = res[64:]
-
     U = (slice(0, 2), slice(2, 4))
 
-    def send_a(q):
-        return [go(f"a{q}{s}", sa.at[q, U[s]], ra.at[q, U[s]], zs[s]) for s in range(2)]
-
-    def send_b(q, s, half):
-        return go(f"b{q}{s}{half}", sb.at[s, q, U[half]], rb.at[s, q, U[half]], zs[s])
-
-    got_a = [send_a(0), None]
+    def pass_y(name, got, relay, dst):
+        out = []
+        for s in range(2):
+            got[s].wait_recv()
+            out.append(go(f"{name}p{s}", relay.at[s], dst(s), ys[s]))
+        return out
+
+    got_yf = []
+    for uv in range(4):
+        got_wt[uv].wait_recv()
+        res = term(2, uv)
+        sf[uv] = res[:64].astype(BF16)
+        farp[uv] = res[64:]
+        if uv % 2 == 1:
+            s = uv // 2
+            got_yf.append(go(f"yf{s}", sf.at[U[s]], ryf.at[s], ys[s]))
 
     @pl.loop(0, 2)
     def _(k):
         for s, step in enumerate((1, 3)):
             res = term(step, 2 * s + k)
-            part[s, 0, k] = res[:64]
-            part[s, 1, k] = res[64:]
+            sb[s, 0, 2 * s + k] = res[:64].astype(BF16)
+            part[s, k] = res[64:]
             res = term(step, 2 - 2 * s + k).astype(BF16)
             sb[s, 0, 2 - 2 * s + k] = res[:64]
             sb[s, 1, 2 - 2 * s + k] = res[64:]
 
-    got_b = [[], []]
-    got_b[0] += [send_b(0, s, 1 - s) for s in range(2)]
-
-    def add_a(q):
-        for s in range(2):
-            got_a[q][s].wait_recv()
-            sb[s, q, U[s]] = (part[s, q] + ra[q, U[s]].astype(F32)).astype(BF16)
-            got_b[q].append(send_b(q, s, s))
+    got_b0 = [go(f"b0{s}", sb.at[s, 0], rb.at[s, 0], zs[s]) for s in range(2)]
+
+    def send_b(s, half):
+        return go(f"b1{s}{half}", sb.at[s, 1, U[half]], rb.at[s, 1, U[half]], zs[s])
+
+    got_b1 = [send_b(s, 1 - s) for s in range(2)]
 
     loads[3].wait()
     pre[...] = jnp.dot(pp[0], wv[...], preferred_element_type=F32)
@@ -296,9 +296,7 @@
     stat[0] = across(pick_lane(mean, lane_sum(total)), 8)
     got_stat = [go(f"stat{k}", stat.at[0], stat.at[k], mpk[k - 1]) for k in (1, 2, 3)]
 
-    add_a(0)
-    got_a[1] = send_a(1)
-    got_b[1] += [send_b(1, s, 1 - s) for s in range(2)]
+    got_f1 = pass_y("yf", got_yf, ryf, lambda s: rf.at[U[s]])
 
     @pl.loop(0, 4)
     def _(uv):
@@ -347,34 +345,17 @@
     def to_mate(slot, half=None):
         return go(f"m{slot}{half}", spot(slot, half), spot(slot + 1, half), mate)
 
-    def over_y(name, src, relay):
-        return [go(f"{name}{s}", src(s), relay.at[s], ys[s]) for s in range(2)]
-
-    def pass_y(name, got, relay, dst):
-        out = []
-        for s in range(2):
-            got[s].wait_recv()
-            out.append(go(f"{name}p{s}", relay.at[s], dst(s), ys[s]))
-        return out
-
-    got_ya = over_y("ya", lambda s: spot(0, s), rya)
     got_mate = [to_mate(0)]
 
-    for copy in got_b[0]:
+    for copy in got_b0:
         copy.wait_recv()
     sc[...] = (own[0] + rb[0, 0].astype(F32) + rb[1, 0].astype(F32)).astype(BF16)
-    got_yc = over_y("yc", lambda s: sc.at[U[s]], ryc)
-    got_flip = pass_y("ya", got_ya, rya, lambda s: spot(2, s))
-    add_a(1)
-
-    def spread(slot):
-        return [
-            go(f"z{slot}0", spot(slot), spot(slot + 12), zs[0]),
-            go(f"z{slot}1", spot(slot), spot(slot + 4), zs[1]),
-        ]
-
-    got_z = spread(0)
-    got_pp = go("pp", pp.at[0], pp.at[1], mate)
+    got_yc = [go(f"yc{s}", sc.at[U[s]], ryc.at[s], ys[s]) for s in range(2)]
+    got_a = []
+    for s in range(2):
+        got_f1[s].wait_recv()
+        sa[U[s]] = (farp[U[s]] + rf[U[s]].astype(F32)).astype(BF16)
+        got_a.append(go(f"a{s}", sa.at[U[s]], ra.at[U[s]], zs[s]))
 
     r = lax.broadcasted_iota(jnp.int32, (512, W), 0)
     ch = lax.broadcasted_iota(jnp.int32, (512, W), 1)
@@ -387,12 +368,27 @@
     upt[...] = jnp.transpose(upr[...].astype(F32)).astype(BF16)
 
     got_c = pass_y("yc", got_yc, ryc, lambda s: rc.at[U[s]])
-    for copy in got_flip:
-        copy.wait_recv()
-    got_zf = spread(2)
-    got_mate.append(to_mate(2))
-
-    for copy in got_b[1]:
+    got_ya = [go(f"ya{s}", spot(0, s), rya.at[s], ys[s]) for s in range(2)]
+    last = []
+    for s in range(2):
+        got_a[s].wait_recv()
+        sb[s, 1, U[s]] = (part[s] + ra[U[s]].astype(F32)).astype(BF16)
+        last.append(send_b(s, s))
+    got_b1 += last
+
+    def spread(slot):
+        return [
+            go(f"z{slot}0", spot(slot), spot(slot + 12), zs[0]),
+            go(f"z{slot}1", spot(slot), spot(slot + 4), zs[1]),
+        ]
+
+    for copy in last:
+        copy.wait_send()
+    pending[:] = [copy for copy in pending if all(copy is not gone for gone in last)]
+    got_z = spread(0)
+    got_pp = go("pp", pp.at[0], pp.at[1], mate)
+
+    for copy in got_b1:
         copy.wait_recv()
     for uv in range(4):
         own[1, uv] = own[1, uv] + rb[0, 1, uv].astype(F32) + rb[1, 1, uv].astype(F32)
@@ -458,9 +454,9 @@
             got[s].wait_recv()
             got_mate.append(to_mate(slot + 8, s))
 
-    got_f = onward(0, got_z)
-
-    def products(n, first):
+    got_flip = pass_y("ya", got_ya, rya, lambda s: spot(2, s))
+
+    def tube_part(n):
         rows = slice(256 * n, 256 * n + 256)
 
         @pl.loop(0, 4)
@@ -477,12 +473,13 @@
             def _():
                 acc[rows] = acc[rows] + res
 
+    def gwt_part(n, first=False):
+        rows = slice(256 * n, 256 * n + 256)
+
+        @pl.loop(0, 4)
+        def _(uv):
             more = jnp.dot(upt[:, rows], ev[uv, rows], preferred_element_type=F32)
-            gwt[uv] = more if first else gwt[uv] + more
-
-    for copy in got_mate[:2]:
-        copy.wait_recv()
-    products(0, True)
+            gacc[uv] = more if first else gacc[uv] + more
 
     for copy in got_stat:
         copy.wait_recv()
@@ -547,6 +544,9 @@
             for s in range(2)
         ]
         got2[k] = []
+
+    def stage1b(k):
+        h, first, n = PIECES[k]
         for s in range(2):
             near = 128 * ((coord[h] + 1 + 2 * s) % 4)
             rows = slice(64 - 64 * s, 128 - 64 * s)
@@ -618,28 +618,41 @@
             tail = tail[0:16] + tail[64:80]
             for a in range(3):
                 gdw[a] = tail[3 * a : 3 * a + 3, 0:28]
-            ggain[...] = tail[9:10, 0:28]
-            gbias[...] = tail[10:11, 0:28]
-
-    for k in range(4):
+            ggain[...] = tail[9, 0:28]
+            gbias[...] = tail[10, 0:28]
+
+    for copy in got_flip:
+        copy.wait_recv()
+    got_zf = spread(2)
+    got_mate.append(to_mate(2))
+    for k in (1, 0, 2, 3):
         stage1(k)
+    for k in (1, 0, 2, 3):
+        stage1b(k)
+    got_f = onward(0, got_z)
+    for copy in got_mate[:2]:
+        copy.wait_recv()
+    tube_part(0)
+    gwt_part(0, True)
+    for k in (1, 0, 2, 3):
+        stage2(k)
     gather_end(0, got_f)
     got_ff = onward(2, got_zf)
-    for k in range(4):
-        stage2(k)
     for copy in got_mate[2:8]:
         copy.wait_recv()
-    products(3, False)
-    products(1, False)
+    tube_part(3)
+    gwt_part(3)
+    stage3(1)
     stage3(0)
-    stage3(1)
+    tube_part(1)
+    gwt_part(1)
     gather_end(2, got_ff)
     stage3(2)
+    stage4(1)
     stage4(0)
-    stage4(1)
     for copy in got_mate[8:]:
         copy.wait_recv()
-    products(2, False)
+    tube_part(2)
 
     for k in range(8):
         piece = jnp.concatenate([acc[64 * s + 8 * k : 64 * s + 8 * k + 8] for s in range(16)], axis=0)
@@ -647,9 +660,12 @@
     got_t = [go(f"t{k}", ts.at[d], tr.at[k], dev) for k, (d, dev) in enumerate(peers)]
     stage3(3)
     stage4(2)
+    gwt_part(2)
+    keep = pltpu.make_async_copy(gacc, gwt, load.at[4])
+    keep.start()
+    stage4(3)
+    stage5(1)
     stage5(0)
-    stage5(1)
-    stage4(3)
     for copy in got_t:
         copy.wait_recv()
     tot = ts[dest].astype(F32)
@@ -661,6 +677,7 @@
     stage5(3)
     for copy in pending:
         copy.wait_send()
+    keep.wait()
 
 
 def run_main(frames, batch, patches, w_in, wt, gout, gain, bias, dw):
@@ -671,26 +688,26 @@
         main_kernel,
         out_shape=(
             sds((16, 8, OW), BF16), sds((28, D), F32), sds((3, 3, 28), F32),
-            sds((1, 28), F32), sds((1, 28), F32), sds((4, OW, W), F32),
+            sds((28,), F32), sds((28,), F32), sds((4, OW, W), F32),
         ),
         in_specs=[SMEM, SMEM, ANY, ANY, ANY, ANY, VMEM, VMEM, VMEM],
-        out_specs=(VMEM,) * 6,
+        out_specs=(VMEM, VMEM, VMEM, VMEM, VMEM, ANY),
         scratch_shapes=[
             vm((TOK, D), BF16), vm((2, TOK, D), BF16), vm((D, W), BF16),
             vm((4, OW, W), BF16), vm((4, OW, W), BF16),
             vm((16, 64, OW), BF16), vm((16, 64, OW), BF16), vm((16, OW), F32),
             vm((1024, OW), BF16), vm((4, 128, OW), BF16), vm((1, W), F32), vm((1, W), F32),
-            vm((2, *blk), BF16), vm((2, *blk), BF16), vm((2, 2, *half), F32),
+            vm(blk, BF16), vm(blk, BF16), vm(blk, F32), vm(blk, BF16), vm(blk, BF16), vm((2, *half), F32),
             vm((2, 2, *blk), BF16), vm((2, 2, *blk), BF16), vm((2, *blk), F32),
-            vm(blk, BF16), vm(blk, BF16), vm((2, *half), BF16), vm((2, *half), BF16),
+            vm(blk, BF16), vm(blk, BF16), *[vm((2, *half), BF16)] * 3,
             *[vm((TOK, W), F32)] * 6, vm((16, W), F32), vm((4, 8, TOK), F32), vm((4, 8, TOK), F32),
             vm((4, 1024, W), BF16), vm((2, 512, W), BF16), vm((TOK + LANES, W), BF16),
             vm((2, 512, TOK + LANES), BF16), vm((512, TOK + LANES), BF16),
             vm((4, 128, W), BF16), vm((4, 2, 128, W), BF16), vm((4, 128, W), F32),
             vm((4, 128, W), BF16), vm((4, 32, W), BF16), vm((4, 2, 16, W), BF16),
-            vm((4, 2, 32, W), BF16), vm((1024, OW), F32), vm((OW, 1024), BF16),
+            vm((4, 2, 32, W), BF16), vm((1024, OW), F32), vm((4, OW, W), F32), vm((OW, 1024), BF16),
             vm((8, 128, OW), BF16), vm((7, 128, OW), BF16),
-            DMA((4,)), DMA((NSEM,)), DMA((NSEM,)),
+            DMA((5,)), DMA((NSEM,)), DMA((NSEM,)),
         ],
         compiler_params=pltpu.CompilerParams(
             collective_id=0, has_side_effects=True, vmem_limit_bytes=63 * 1024 * 1024
@@ -699,32 +716,35 @@
     )(frames, batch, patches, w_in, wt, gout, gain, bias, dw)
 
 
-def out_kernel(a, b, c, d, e, big, ao, bo, co, do, eo, bigo, buf, sem):
-    ins = [pltpu.make_async_copy(big.at[k], buf.at[k], sem.at[0, k]) for k in range(4)]
-    outs = [pltpu.make_async_copy(buf.at[k], bigo.at[k], sem.at[1, k]) for k in range(4)]
-    for copy in ins:
+CUTS = 8
+
+
+def out_kernel(*refs):
+    n = 6
+    srcs, outs, bufs, sem = refs[:n], refs[n : 2 * n], refs[2 * n : 3 * n], refs[3 * n]
+    parts = [(a, b, c) for a, b, c in zip(srcs[:5], outs[:5], bufs[:5])]
+    rows = OW // (CUTS // 4)
+    for k in range(CUTS):
+        at = (k * 4 // CUTS, slice(k % (CUTS // 4) * rows, k % (CUTS // 4) * rows + rows))
+        parts.append((srcs[5].at[at], outs[5].at[at], bufs[5].at[at]))
+    there = [pltpu.make_async_copy(a, c, sem.at[0, k]) for k, (a, b, c) in enumerate(parts)]
+    back = [pltpu.make_async_copy(c, b, sem.at[1, k]) for k, (a, b, c) in enumerate(parts)]
+    for copy in there[5:] + there[:5]:
         copy.start()
-    for src, dst in ((a, ao), (b, bo), (c, co)):
-        dst[...] = src[...]
-    do[...] = d[...].reshape(28)
-    eo[...] = e[...].reshape(28)
-    for k in range(4):
-        ins[k].wait()
-        outs[k].start()
-    for k in range(4):
-        outs[k].wait()
+    for k in (*range(5, 5 + CUTS), *range(5)):
+        there[k].wait()
+        back[k].start()
+    for copy in back:
+        copy.wait()
 
 
 def run_out(*arrays):
-    sds = jax.ShapeDtypeStruct
-    shapes = [sds(x.shape, x.dtype) for x in arrays]
-    shapes[3] = shapes[4] = sds((28,), F32)
     return pl.pallas_call(
         out_kernel,
-        out_shape=tuple(shapes),
-        in_specs=[VMEM] * 5 + [ANY],
-        out_specs=tuple([VMEM] * 5 + [ANY]),
-        scratch_shapes=[pltpu.VMEM((4, OW, W), F32), DMA((2, 4))],
+        out_shape=tuple(jax.ShapeDtypeStruct(x.shape, x.dtype) for x in arrays),
+        in_specs=[ANY] * 6,
+        out_specs=(ANY,) * 6,
+        scratch_shapes=[*[pltpu.VMEM(x.shape, x.dtype) for x in arrays], DMA((2, 5 + CUTS))],
         name="out",
     )(*arrays)
 

time: 108 us -> 101 us (0.935)
  Pallas kernels: 107 us -> 100 us
    pallas_call x1, Pallas kernels: 102 us -> 97.2 us  [run_main(): pl.pallas_call(main_kernel, out_shape=(sds((16, 8, OW), BF16), sds((28, D...]
    pallas_call x1, Pallas kernels: 4.66 us -> 3.23 us  [run_out(): pl.pallas_call(out_kernel, out_shape=tuple((jax.ShapeDtypeStruct(x.shape,...]
where the time goes in v1:
time: 101 us
  Pallas kernels  100 us (99%)
    pallas_call x1, Pallas kernels, run_main(): pl.pallas_call(main_kernel, out_shape=(sds((16, 8, OW), BF16), sds((28, D...  97.2 us
    pallas_call x1, Pallas kernels, run_out(): pl.pallas_call(out_kernel, out_shape=tuple((jax.ShapeDtypeStruct(x.shape,...  3.23 us

profile of v1, /device:TPU:0, one launch (start us, length us, event | category | flops | bytes accessed | tf_op | source)
XLA Modules:
  0.0 101.0 jit_solution(18213777560825599480)
XLA Ops:
  0.6 97.2 %main.1 = (bf16[16,8,224]{2,1,0:T(8,128)(2,1)}, f32[28,3200]{1,0:T(8,128)}, f32[3,3,28]{2,1,0:T(4,128)}, f32[28]{0:T(128)}, f32[28]{0:T(128)}, /*index=5*/f32[4,224,896]{2,1,0:T(8,128)}) custom-call(s32[16]{0:T(128)} %frames.1, s32[16]{0:T(128)} %batch.1, bf16[256,3200]{1,0:T(8,128)(2,1)} %bitcast.8, bf16[3200,896]{1,0:T(8,128)(2,1)} %w_in.1, ...), custom_call_target="tpu_custom_call" | custom-call | tf_op jit(solution)/shard_map/main/pallas_call | solution.py:687
  97.8 3.2 %out.1 = (bf16[16,8,224]{2,1,0:T(8,128)(2,1)}, f32[28,3200]{1,0:T(8,128)}, f32[3,3,28]{2,1,0:T(4,128)}, f32[28]{0:T(128)}, f32[28]{0:T(128)}, /*index=5*/f32[4,224,896]{2,1,0:T(8,128)}) custom-call(bf16[16,8,224]{2,1,0:T(8,128)(2,1)} %get-tuple-element.18.refs_0_, f32[28,3200]{1,0:T(8,128)} %get-tuple-element.19.refs_1_, ...), custom_call_target="tpu_custom_call" | custom-call | tf_op jit(solution)/shard_map/out/pallas_call | solution.py:742

commit v2 on v1

--- a/solution.py
+++ b/solution.py
@@ -139,9 +139,9 @@
 DMA = pltpu.SemaphoreType.DMA
 
 
-PIECES = ((0, 0, 896), (1, 896, 896), (1, 1792, 768), (1, 2560, 768))
+PIECES = ((0, 0, 640), (1, 640, 896), (1, 1536, 896), (1, 2432, 896))
 GROUPS = (0, 3, 1, 2)
-NSEM = 128
+NSEM = 113
 
 
 def ds(start, size, align):
@@ -156,6 +156,7 @@
     pre, normed, act, slope, mslope, gmaps, small, stat, stat2,
     ev, sub, gp, left, leftr,
     ra2, rb2, own2, ownb, tra, tb, trb, acc, gacc, upt, ts, tr,
+    tubesv, gwinv, gdwv, ggainv, gbiasv,
     load, send, recv,
 ):
     me = Place()
@@ -255,32 +256,30 @@
             out.append(go(f"{name}p{s}", relay.at[s], dst(s), ys[s]))
         return out
 
-    got_yf = []
     for uv in range(4):
         got_wt[uv].wait_recv()
+        for s, step in enumerate((1, 3)):
+            res = term(step, uv)
+            sb[s, 0, uv] = res[:64].astype(BF16)
+            if uv // 2 == s:
+                part[s, uv % 2] = res[64:]
+            else:
+                sb[s, 1, uv] = res[64:].astype(BF16)
+
+    got_b0 = [go(f"b0{s}", sb.at[s, 0], rb.at[s, 0], zs[s]) for s in range(2)]
+
+    def send_b(s, half):
+        return go(f"b1{s}{half}", sb.at[s, 1, U[half]], rb.at[s, 1, U[half]], zs[s])
+
+    got_b1 = [send_b(s, 1 - s) for s in range(2)]
+
+    @pl.loop(0, 4)
+    def _(uv):
         res = term(2, uv)
         sf[uv] = res[:64].astype(BF16)
         farp[uv] = res[64:]
-        if uv % 2 == 1:
-            s = uv // 2
-            got_yf.append(go(f"yf{s}", sf.at[U[s]], ryf.at[s], ys[s]))
-
-    @pl.loop(0, 2)
-    def _(k):
-        for s, step in enumerate((1, 3)):
-            res = term(step, 2 * s + k)
-            sb[s, 0, 2 * s + k] = res[:64].astype(BF16)
-            part[s, k] = res[64:]
-            res = term(step, 2 - 2 * s + k).astype(BF16)
-            sb[s, 0, 2 - 2 * s + k] = res[:64]
-            sb[s, 1, 2 - 2 * s + k] = res[64:]
-
-    got_b0 = [go(f"b0{s}", sb.at[s, 0], rb.at[s, 0], zs[s]) for s in range(2)]
-
-    def send_b(s, half):
-        return go(f"b1{s}{half}", sb.at[s, 1, U[half]], rb.at[s, 1, U[half]], zs[s])
-
-    got_b1 = [send_b(s, 1 - s) for s in range(2)]
+
+    got_yf = [go(f"yf{s}", sf.at[U[s]], ryf.at[s], ys[s]) for s in range(2)]
 
     loads[3].wait()
     pre[...] = jnp.dot(pp[0], wv[...], preferred_element_type=F32)
@@ -439,6 +438,8 @@
     stat2[0] = across(pick_lane(lane_sum(one), lane_sum(two)), 8)
     got_stat = [go(f"back{k}", stat2.at[0], stat2.at[k], mpk[k - 1]) for k in (1, 2, 3)]
 
+    got_flip = pass_y("ya", got_ya, rya, lambda s: spot(2, s))
+
     def onward(slot, got):
         out = []
         got[0].wait_recv()
@@ -453,8 +454,6 @@
         for s in range(2):
             got[s].wait_recv()
             got_mate.append(to_mate(slot + 8, s))
-
-    got_flip = pass_y("ya", got_ya, rya, lambda s: spot(2, s))
 
     def tube_part(n):
         rows = slice(256 * n, 256 * n + 256)
@@ -509,6 +508,11 @@
     left[1] = turn(1)
     got_left = go("left", left.at[1], leftr, mate)
     left[0] = turn(0)
+    got_f = onward(0, got_z)
+    for copy in got_flip:
+        copy.wait_recv()
+    got_zf = spread(2)
+    got_mate.append(to_mate(2))
     got_pp.wait_recv()
     got_left.wait_recv()
 
@@ -521,6 +525,13 @@
 
     def sb_at(k, s, b, size):
         return wv.at[2048 + 128 * k + 64 * s + b : 2048 + 128 * k + 64 * s + b + size, 0 : PIECES[k][2]]
+
+    finals = []
+
+    def done(src, dst):
+        copy = pltpu.make_async_copy(src, dst, load.at[4 + len(finals)])
+        copy.start()
+        finals.append(copy)
 
     def stage1(k):
         h, first, n = PIECES[k]
@@ -612,72 +623,87 @@
         val = own2[k, ds(32 * coord[1 - h], 32, 32), 0:n]
         val = val + trb[k, 0, :, 0:n].astype(F32) + trb[k, 1, :, 0:n].astype(F32)
         grad = min(first + n, D) - first
-        gwin[:, first : first + grad] = val[0:28, 0:grad]
+        gwinv[:, first : first + grad] = val[0:28, 0:grad]
+        done(gwinv.at[:, first : first + grad], gwin.at[:, first : first + grad])
         if grad < n:
             tail = jnp.transpose(jnp.concatenate([val[:, grad:], jnp.zeros((96, LANES), F32)], axis=0))
             tail = tail[0:16] + tail[64:80]
             for a in range(3):
-                gdw[a] = tail[3 * a : 3 * a + 3, 0:28]
-            ggain[...] = tail[9, 0:28]
-            gbias[...] = tail[10, 0:28]
-
-    for copy in got_flip:
-        copy.wait_recv()
-    got_zf = spread(2)
-    got_mate.append(to_mate(2))
-    for k in (1, 0, 2, 3):
+                gdwv[a] = tail[3 * a : 3 * a + 3, 0:28]
+            ggainv[...] = tail[9, 0:28]
+            gbiasv[...] = tail[10, 0:28]
+            done(gdwv, gdw)
+            done(ggainv, ggain)
+            done(gbiasv, gbias)
+
+    for k in (1, 2, 3):
         stage1(k)
-    for k in (1, 0, 2, 3):
+    for k in (1, 2, 3):
         stage1b(k)
-    got_f = onward(0, got_z)
-    for copy in got_mate[:2]:
-        copy.wait_recv()
-    tube_part(0)
+    stage1(0)
+    stage1b(0)
+    got_t = []
+
+    def tubes_put(n):
+        tube_part(n)
+        at = 32 * GROUPS.index(n)
+        for k in range(8):
+            piece = jnp.concatenate(
+                [acc[64 * s + 8 * k : 64 * s + 8 * k + 8] for s in range(4 * n, 4 * n + 4)], axis=0
+            )
+            ts[k, at : at + 32] = piece.astype(BF16)
+
+    def tubes_send(name, rows):
+        for k, (d, dev) in enumerate(peers):
+            got_t.append(go(f"{name}{k}", ts.at[d, rows], tr.at[k, rows], dev))
+
+    for copy in (got_mate[0], got_mate[3]):
+        copy.wait_recv()
+    tubes_put(0)
     gwt_part(0, True)
-    for k in (1, 0, 2, 3):
-        stage2(k)
+    stage2(1)
+    stage2(2)
+    stage2(3)
+    got_ff = onward(2, got_zf)
+    stage2(0)
+    for copy in (*got_mate[1:3], *got_mate[4:6]):
+        copy.wait_recv()
+    tubes_put(3)
+    tubes_put(1)
+    tubes_send("t", slice(0, 96))
     gather_end(0, got_f)
-    got_ff = onward(2, got_zf)
-    for copy in got_mate[2:8]:
-        copy.wait_recv()
-    tube_part(3)
     gwt_part(3)
+    gwt_part(1)
     stage3(1)
-    stage3(0)
-    tube_part(1)
-    gwt_part(1)
     gather_end(2, got_ff)
     stage3(2)
+    stage3(3)
+    stage3(0)
     stage4(1)
-    stage4(0)
-    for copy in got_mate[8:]:
-        copy.wait_recv()
-    tube_part(2)
-
-    for k in range(8):
-        piece = jnp.concatenate([acc[64 * s + 8 * k : 64 * s + 8 * k + 8] for s in range(16)], axis=0)
-        ts[k] = piece.astype(BF16)
-    got_t = [go(f"t{k}", ts.at[d], tr.at[k], dev) for k, (d, dev) in enumerate(peers)]
-    stage3(3)
-    stage4(2)
+    for copy in got_mate[6:]:
+        copy.wait_recv()
+    tubes_put(2)
+    tubes_send("u", slice(96, 128))
+    for k in (2, 3, 0):
+        stage4(k)
     gwt_part(2)
-    keep = pltpu.make_async_copy(gacc, gwt, load.at[4])
-    keep.start()
-    stage4(3)
-    stage5(1)
-    stage5(0)
+    done(gacc, gwt)
+    for k in (1, 2, 3, 0):
+        stage5(k)
     for copy in got_t:
         copy.wait_recv()
     tot = ts[dest].astype(F32)
     for k in range(7):
         tot = tot + tr[k].astype(F32)
     for s in range(16):
-        tubes[pair_of(s)] = tot[8 * s : 8 * s + 8].astype(BF16)
-    stage5(2)
-    stage5(3)
+        at = 32 * GROUPS.index(s // 4) + 8 * (s % 4)
+        tubesv[pair_of(s)] = tot[at : at + 8].astype(BF16)
+    done(tubesv, tubes)
     for copy in pending:
         copy.wait_send()
-    keep.wait()
+    for copy in finals:
+        copy.wait()
+    assert len(number) == NSEM, len(number)
 
 
 def run_main(frames, batch, patches, w_in, wt, gout, gain, bias, dw):
@@ -691,7 +717,7 @@
             sds((28,), F32), sds((28,), F32), sds((4, OW, W), F32),
         ),
         in_specs=[SMEM, SMEM, ANY, ANY, ANY, ANY, VMEM, VMEM, VMEM],
-        out_specs=(VMEM, VMEM, VMEM, VMEM, VMEM, ANY),
+        out_specs=(ANY,) * 6,
         scratch_shapes=[
             vm((TOK, D), BF16), vm((2, TOK, D), BF16), vm((D, W), BF16),
             vm((4, OW, W), BF16), vm((4, OW, W), BF16),
@@ -707,7 +733,8 @@
             vm((4, 128, W), BF16), vm((4, 32, W), BF16), vm((4, 2, 16, W), BF16),
             vm((4, 2, 32, W), BF16), vm((1024, OW), F32), vm((4, OW, W), F32), vm((OW, 1024), BF16),
             vm((8, 128, OW), BF16), vm((7, 128, OW), BF16),
-            DMA((5,)), DMA((NSEM,)), DMA((NSEM,)),
+            vm((16, 8, OW), BF16), vm((28, D), F32), vm((3, 3, 28), F32), vm((28,), F32), vm((28,), F32),
+            DMA((13,)), DMA((NSEM,)), DMA((NSEM,)),
         ],
         compiler_params=pltpu.CompilerParams(
             collective_id=0, has_side_effects=True, vmem_limit_bytes=63 * 1024 * 1024

time: 101 us -> 93.5 us (0.926)
  Pallas kernels: 100 us -> 92.7 us
    pallas_call x1, Pallas kernels: 97.2 us -> 89.4 us  [run_main(): pl.pallas_call(main_kernel, out_shape=(sds((16, 8, OW), BF16), sds((28, D...]
where the time goes in v2:
time: 93.5 us; the launch traced here: 93.3 us
  Pallas kernels  92.7 us (99%)
    pallas_call x1, Pallas kernels, run_main(): pl.pallas_call(main_kernel, out_shape=(sds((16, 8, OW), BF16), sds((28, D...  89.4 us
    pallas_call x1, Pallas kernels, run_out(): pl.pallas_call(out_kernel, out_shape=tuple((jax.ShapeDtypeStruct(x.shape,...  3.23 us

profile of v2, /device:TPU:0, one launch (start us, length us, event | category | flops | bytes accessed | tf_op | source)
XLA Modules:
  0.0 93.3 jit_solution(2409710837080753517)
XLA Ops:
  0.6 89.4 %main.1 = (bf16[16,8,224]{2,1,0:T(8,128)(2,1)}, f32[28,3200]{1,0:T(8,128)}, f32[3,3,28]{2,1,0:T(4,128)}, f32[28]{0:T(128)}, f32[28]{0:T(128)}, /*index=5*/f32[4,224,896]{2,1,0:T(8,128)}) custom-call(s32[16]{0:T(128)} %frames.1, s32[16]{0:T(128)} %batch.1, bf16[256,3200]{1,0:T(8,128)(2,1)} %bitcast.8, bf16[3200,896]{1,0:T(8,128)(2,1)} %w_in.1, ...), custom_call_target="tpu_custom_call" | custom-call | tf_op jit(solution)/shard_map/main/pallas_call | solution.py:713
  90.1 3.2 %out.1 = (bf16[16,8,224]{2,1,0:T(8,128)(2,1)}, f32[28,3200]{1,0:T(8,128)}, f32[3,3,28]{2,1,0:T(4,128)}, f32[28]{0:T(128)}, f32[28]{0:T(128)}, /*index=5*/f32[4,224,896]{2,1,0:T(8,128)}) custom-call(bf16[16,8,224]{2,1,0:T(8,128)(2,1)} %get-tuple-element.18.refs_0_, f32[28,3200]{1,0:T(8,128)} %get-tuple-element.19.refs_1_, ...), custom_call_target="tpu_custom_call" | custom-call | tf_op jit(solution)/shard_map/out/pallas_call | solution.py:769

commit v3 on v2

--- a/solution.py
+++ b/solution.py
@@ -142,6 +142,7 @@
 PIECES = ((0, 0, 640), (1, 640, 896), (1, 1536, 896), (1, 2432, 896))
 GROUPS = (0, 3, 1, 2)
 NSEM = 113
+NSEND = 73
 
 
 def ds(start, size, align):
@@ -178,14 +179,22 @@
         d = (dest + k) % 8
         peers.append((d, (lax.axis_index("dp"), d // 4, d % 4)))
     greet([mate, *zs, *ys, *[dev for _, dev in peers]])
-    pending, number = [], {}
+    pending, number, free, unused = [], {}, list(range(NSEND)), [NSEND]
 
     def go(name, src, dst, dev):
-        i = number.setdefault(name, len(number))
-        copy = remote(src, dst, send.at[i], recv.at[i], dev)
+        i, k = number.setdefault(name, len(number)), free.pop(0)
+        unused[0] = min(unused[0], len(free))
+        copy = remote(src, dst, send.at[k], recv.at[i], dev)
         copy.start()
-        pending.append(copy)
+        pending.append((k, copy))
         return copy
+
+    def sent(copies):
+        for k, copy in list(pending):
+            if any(copy is one for one in copies):
+                copy.wait_send()
+                free.append(k)
+        pending[:] = [p for p in pending if p[0] not in free]
 
     got_gout = go("gout", gout, goo, mate)
     got_wt = [go(f"wt{k}", wt.at[k], wto.at[k], mate) for k in range(4)]
@@ -381,9 +390,8 @@
             go(f"z{slot}1", spot(slot), spot(slot + 4), zs[1]),
         ]
 
-    for copy in last:
-        copy.wait_send()
-    pending[:] = [copy for copy in pending if all(copy is not gone for gone in last)]
+    sent(last)
+    early = [copy for _, copy in pending if all(copy is not one for one in got_ya)]
     got_z = spread(0)
     got_pp = go("pp", pp.at[0], pp.at[1], mate)
 
@@ -395,6 +403,8 @@
         copy.wait_recv()
     for uv in range(4):
         gmaps[64 * uv : 64 * uv + 64, :] = own[1, uv] + rc[uv].astype(F32)
+
+    sent(early)
 
     @pl.loop(0, NB)
     def _(b):
@@ -668,6 +678,7 @@
     stage2(0)
     for copy in (*got_mate[1:3], *got_mate[4:6]):
         copy.wait_recv()
+    early = [copy for _, copy in pending]
     tubes_put(3)
     tubes_put(1)
     tubes_send("t", slice(0, 96))
@@ -679,6 +690,7 @@
     stage3(2)
     stage3(3)
     stage3(0)
+    sent(early)
     stage4(1)
     for copy in got_mate[6:]:
         copy.wait_recv()
@@ -699,11 +711,11 @@
         at = 32 * GROUPS.index(s // 4) + 8 * (s % 4)
         tubesv[pair_of(s)] = tot[at : at + 8].astype(BF16)
     done(tubesv, tubes)
-    for copy in pending:
+    for _, copy in pending:
         copy.wait_send()
     for copy in finals:
         copy.wait()
-    assert len(number) == NSEM, len(number)
+    assert len(number) == NSEM and unused[0] == 0, (len(number), unused)
 
 
 def run_main(frames, batch, patches, w_in, wt, gout, gain, bias, dw):
@@ -734,7 +746,7 @@
             vm((4, 2, 32, W), BF16), vm((1024, OW), F32), vm((4, OW, W), F32), vm((OW, 1024), BF16),
             vm((8, 128, OW), BF16), vm((7, 128, OW), BF16),
             vm((16, 8, OW), BF16), vm((28, D), F32), vm((3, 3, 28), F32), vm((28,), F32), vm((28,), F32),
-            DMA((13,)), DMA((NSEM,)), DMA((NSEM,)),
+            DMA((13,)), DMA((NSEND,)), DMA((NSEM,)),
         ],
         compiler_params=pltpu.CompilerParams(
             collective_id=0, has_side_effects=True, vmem_limit_bytes=63 * 1024 * 1024

time: 93.5 us -> 93.1 us (level)
  no operation moved by 1% of the time
where the time goes in v3:
time: 93.1 us; the launch traced here: 92.9 us
  Pallas kernels  92.3 us (99%)
    pallas_call x1, Pallas kernels, run_main(): pl.pallas_call(main_kernel, out_shape=(sds((16, 8, OW), BF16), sds((28, D...  89.1 us
    pallas_call x1, Pallas kernels, run_out(): pl.pallas_call(out_kernel, out_shape=tuple((jax.ShapeDtypeStruct(x.shape,...  3.23 us

profile of v3, /device:TPU:0, one launch (start us, length us, event | category | flops | bytes accessed | tf_op | source)
XLA Modules:
  0.0 92.9 jit_solution(6734644912596582686)
XLA Ops:
  0.6 89.1 %main.1 = (bf16[16,8,224]{2,1,0:T(8,128)(2,1)}, f32[28,3200]{1,0:T(8,128)}, f32[3,3,28]{2,1,0:T(4,128)}, f32[28]{0:T(128)}, f32[28]{0:T(128)}, /*index=5*/f32[4,224,896]{2,1,0:T(8,128)}) custom-call(s32[16]{0:T(128)} %frames.1, s32[16]{0:T(128)} %batch.1, bf16[256,3200]{1,0:T(8,128)(2,1)} %bitcast.8, bf16[3200,896]{1,0:T(8,128)(2,1)} %w_in.1, ...), custom_call_target="tpu_custom_call" | custom-call | tf_op jit(solution)/shard_map/main/pallas_call | solution.py:725
  89.7 3.2 %out.1 = (bf16[16,8,224]{2,1,0:T(8,128)(2,1)}, f32[28,3200]{1,0:T(8,128)}, f32[3,3,28]{2,1,0:T(4,128)}, f32[28]{0:T(128)}, f32[28]{0:T(128)}, /*index=5*/f32[4,224,896]{2,1,0:T(8,128)}) custom-call(bf16[16,8,224]{2,1,0:T(8,128)(2,1)} %get-tuple-element.18.refs_0_, f32[28,3200]{1,0:T(8,128)} %get-tuple-element.19.refs_1_, ...), custom_call_target="tpu_custom_call" | custom-call | tf_op jit(solution)/shard_map/out/pallas_call | solution.py:781
